TPU v7x, 32 devices: a whole 2x2x4 slice. The times are simulated.
32 devices in a mesh: row: 4 (over y, x), col: 8 (over z, core).
Axes of the slice: x: 2, y: 2, z: 4, core: 2. Of those that a mesh axis runs over, the one named last changes fastest.
Arguments:
- tokens: bfloat16 [256, 8192], P('col', 'row'), may hold values from -500 to 500
- norm_gain: float32 [8192], P('row'), may hold values from 0.5 to 1.5
- cotangent: bfloat16 [256, 8192], P('col', 'row'), may hold values from -6 to 6
- gate_frozen_weight: bfloat16 [8192, 28672], P('row', 'col'), may hold values from -0.0625 to 0.0625
- up_frozen_weight: bfloat16 [8192, 28672], P('row', 'col'), may hold values from -0.0625 to 0.0625
- down_frozen_weight: bfloat16 [28672, 8192], P('col', 'row'), may hold values from -0.03125 to 0.03125
- gate_input_factor: bfloat16 [8192, 64], P('row'), may hold values from -0.0625 to 0.0625
- gate_output_factor: bfloat16 [64, 28672], P(None, 'col'), may hold values from -0.75 to 0.75
- up_input_factor: bfloat16 [8192, 64], P('row'), may hold values from -0.0625 to 0.0625
- up_output_factor: bfloat16 [64, 28672], P(None, 'col'), may hold values from -0.75 to 0.75
- down_input_factor: bfloat16 [28672, 64], P('col'), may hold values from -0.03125 to 0.03125
- down_b: bfloat16 [64, 8192], P(None, 'row'), may hold values from -0.75 to 0.75
- gate_input_factor_direction: bfloat16 [8192, 64], P('row'), may hold values from -0.0625 to 0.0625
- gate_output_factor_direction: bfloat16 [64, 28672], P(None, 'col'), may hold values from -0.75 to 0.75
- up_input_factor_direction: bfloat16 [8192, 64], P('row'), may hold values from -0.0625 to 0.0625
- up_output_factor_direction: bfloat16 [64, 28672], P(None, 'col'), may hold values from -0.75 to 0.75
- down_input_factor_direction: bfloat16 [28672, 64], P('col'), may hold values from -0.03125 to 0.03125
- down_b_dir: bfloat16 [64, 8192], P(None, 'row'), may hold values from -0.75 to 0.75
Outputs:
- normed_feature_adjoint: float32 [256, 8192], P('col', 'row')
- normed_feature_adjoint_direction: float32 [256, 8192], P('col', 'row')
- curvature_gate_input: float32 [8192, 64], P('row')
- curvature_gate_output: float32 [64, 28672], P(None, 'col')
- curvature_up_input: float32 [8192, 64], P('row')
- curvature_up_output: float32 [64, 28672], P(None, 'col')
- curvature_down_input: float32 [28672, 64], P('col')
- curvature_down_output: float32 [64, 8192], P(None, 'row')
All inputs are finite; a program needn't handle non-finite values.
Results may differ from a plain program's by a relative error of at most 0.024.
Values may be sent and summed in bfloat16 or wider, within the bound.
A program may use at most 128 MiB of HBM per device.

v0:
```python
import jax
import jax.numpy as jnp
from jax import lax
from jax.sharding import PartitionSpec as P

D = 8192
adapter_scale = 0.5
epsilon = 1e-05


def curvature_product(left, right):
    return jnp.dot(left, right, preferred_element_type=jnp.float32)


def cross_shard_total(left, right):
    return lax.dot_general(
        left, right, (((1,), (1,)), ((), ())), preferred_element_type=jnp.float32
    )


def summed_over_rows(left, right):
    return lax.dot_general(
        left, right, (((0,), (0,)), ((), ())), preferred_element_type=jnp.float32
    )


def lowered(factor, panel):
    return lax.dot_general(
        factor, panel, (((0,), (1,)), ((), ())), preferred_element_type=jnp.float32
    )


def lifted(adjoint, factor):
    return lax.dot_general(
        adjoint, factor, (((0,), (1,)), ((), ())), precision=lax.Precision.HIGHEST
    )


def second_order(
    gate_preactivation,
    up_preactivation,
    hidden_adjoint,
    gate_tangent_rows,
    up_tangent_rows,
    adjoint_tangent_rows,
):
    sigma = jax.nn.sigmoid(gate_preactivation)
    silu_value = gate_preactivation * sigma
    slope = sigma * (1.0 + gate_preactivation * (1.0 - sigma))
    bend = sigma * (1.0 - sigma) * (2.0 + gate_preactivation * (1.0 - 2.0 * sigma))
    hidden_activation = (silu_value * up_preactivation).astype(jnp.bfloat16)
    hidden_direction = (
        slope * gate_tangent_rows * up_preactivation + silu_value * up_tangent_rows
    ).astype(jnp.bfloat16)
    gate_derivative = (hidden_adjoint * up_preactivation * slope).astype(jnp.bfloat16)
    up_derivative = (hidden_adjoint * silu_value).astype(jnp.bfloat16)
    gate_derivative_direction = (
        adjoint_tangent_rows * up_preactivation * slope
        + hidden_adjoint * (up_tangent_rows * slope + up_preactivation * bend * gate_tangent_rows)
    ).astype(jnp.bfloat16)
    up_derivative_direction = (
        adjoint_tangent_rows * silu_value + hidden_adjoint * slope * gate_tangent_rows
    ).astype(jnp.bfloat16)
    return (
        hidden_activation,
        hidden_direction,
        gate_derivative,
        up_derivative,
        gate_derivative_direction,
        up_derivative_direction,
    )


def on_device(
    tokens,
    norm_gain,
    cotangent,
    gate_frozen_weight,
    up_frozen_weight,
    down_frozen_weight,
    gate_input_factor,
    gate_output_factor,
    up_input_factor,
    up_output_factor,
    down_input_factor,
    down_b,
    gate_input_factor_direction,
    gate_output_factor_direction,
    up_input_factor_direction,
    up_output_factor_direction,
    down_input_factor_direction,
    down_b_dir,
):
    rank_size = gate_input_factor.shape[1]
    width_rows = gate_frozen_weight.shape[0]
    width_columns = gate_frozen_weight.shape[1]
    own_count = tokens.shape[0]
    tokens_f = tokens.astype(jnp.float32)
    squares = lax.psum(jnp.sum(tokens_f * tokens_f, axis=1), "row")
    own_normed = (tokens_f * lax.rsqrt(squares[:, None] / D + epsilon) * norm_gain).astype(
        jnp.bfloat16
    )
    normed_tokens, cot_panel = (
        lax.all_gather(own_normed, "col", axis=0, tiled=True),
        lax.all_gather(cotangent, "col", axis=0, tiled=True),
    )
    in_factors = jnp.concatenate(
        [
            gate_input_factor,
            up_input_factor,
            gate_input_factor_direction,
            up_input_factor_direction,
        ],
        axis=1,
    )
    out_factors = jnp.concatenate([down_b, down_b_dir], axis=0)
    projected = jnp.concatenate(
        [curvature_product(normed_tokens, in_factors), cross_shard_total(cot_panel, out_factors)],
        axis=1,
    )
    ranks = lax.psum(projected, "row").astype(jnp.bfloat16)
    swiglu_block = lax.psum(
        jnp.concatenate(
            [
                curvature_product(normed_tokens, gate_frozen_weight),
                curvature_product(normed_tokens, up_frozen_weight),
                cross_shard_total(cot_panel, down_frozen_weight),
            ],
            axis=1,
        ),
        "row",
    )

    def column(array, index):
        return array[:, index * rank_size : (index + 1) * rank_size]

    (
        gate_rank_rows,
        up_rank_rows,
        gate_rank_rows_direction,
        up_rank_rows_direction,
        adjoint_rank_rows,
        adjoint_rank_rows_direction,
    ) = [column(ranks, index) for index in range(6)]
    gate_preactivation = swiglu_block[:, :width_columns] + adapter_scale * curvature_product(
        gate_rank_rows, gate_output_factor
    )
    up_preactivation = swiglu_block[
        :, width_columns : 2 * width_columns
    ] + adapter_scale * curvature_product(up_rank_rows, up_output_factor)
    hidden_adjoint = swiglu_block[:, 2 * width_columns :] + adapter_scale * cross_shard_total(
        adjoint_rank_rows, down_input_factor
    )
    gate_tangent_rows = adapter_scale * (
        curvature_product(gate_rank_rows_direction, gate_output_factor)
        + curvature_product(gate_rank_rows, gate_output_factor_direction)
    )
    up_tangent_rows = adapter_scale * (
        curvature_product(up_rank_rows_direction, up_output_factor)
        + curvature_product(up_rank_rows, up_output_factor_direction)
    )
    adjoint_tangent_rows = adapter_scale * (
        cross_shard_total(adjoint_rank_rows_direction, down_input_factor)
        + cross_shard_total(adjoint_rank_rows, down_input_factor_direction)
    )
    (
        hidden_activation,
        hidden_direction,
        gate_derivative,
        up_derivative,
        gate_derivative_direction,
        up_derivative_direction,
    ) = second_order(
        gate_preactivation,
        up_preactivation,
        hidden_adjoint,
        gate_tangent_rows,
        up_tangent_rows,
        adjoint_tangent_rows,
    )
    (
        gate_full_rows,
        up_full_rows,
        gate_full_rows_direction,
        up_full_rows_direction,
        adjoint_full_rows,
        adjoint_full_rows_direction,
    ) = [column(ranks, index) for index in range(6)]
    curvature_gate_output = adapter_scale * (
        summed_over_rows(gate_full_rows_direction, gate_derivative)
        + summed_over_rows(gate_full_rows, gate_derivative_direction)
    )
    curvature_up_output = adapter_scale * (
        summed_over_rows(up_full_rows_direction, up_derivative)
        + summed_over_rows(up_full_rows, up_derivative_direction)
    )
    curvature_down_input = adapter_scale * (
        summed_over_rows(hidden_direction, adjoint_full_rows)
        + summed_over_rows(hidden_activation, adjoint_full_rows_direction)
    )
    rank_adjoints = jnp.concatenate(
        [
            cross_shard_total(gate_output_factor, gate_derivative),
            cross_shard_total(up_output_factor, up_derivative),
            cross_shard_total(gate_output_factor, gate_derivative_direction)
            + cross_shard_total(gate_output_factor_direction, gate_derivative),
            cross_shard_total(up_output_factor, up_derivative_direction)
            + cross_shard_total(up_output_factor_direction, up_derivative),
            lowered(down_input_factor, hidden_direction)
            + lowered(down_input_factor_direction, hidden_activation),
        ],
        axis=0,
    )
    factors_f = [
        factor.astype(jnp.float32)
        for factor in (
            gate_input_factor,
            up_input_factor,
            gate_input_factor_direction,
            up_input_factor_direction,
        )
    ]
    normed_f = normed_tokens.astype(jnp.float32)
    cotangent_float = cot_panel.astype(jnp.float32)
    adjoints = lax.psum(rank_adjoints.astype(jnp.bfloat16), "col").astype(jnp.float32)
    adjoint_contribution = cross_shard_total(
        gate_derivative, gate_frozen_weight
    ) + cross_shard_total(up_derivative, up_frozen_weight)
    tangent_contribution = cross_shard_total(
        gate_derivative_direction, gate_frozen_weight
    ) + cross_shard_total(up_derivative_direction, up_frozen_weight)
    adjoint_contribution, tangent_contribution = (adjoint_contribution, tangent_contribution)
    summed = lax.psum_scatter(
        jnp.concatenate([adjoint_contribution, tangent_contribution], axis=1).astype(jnp.bfloat16),
        "col",
        scatter_dimension=0,
        tiled=True,
    ).astype(jnp.float32)
    normed_feature_adjoint = summed[:, :width_rows]
    normed_feature_adjoint_direction = summed[:, width_rows:]
    piece = lax.dynamic_slice_in_dim(adjoints, lax.axis_index("col") * own_count, own_count, 1)
    parts = [piece[index * rank_size : (index + 1) * rank_size] for index in range(5)]
    adjoint_contribution = lifted(parts[0], factors_f[0]) + lifted(parts[1], factors_f[1])
    tangent_contribution = (
        lifted(parts[2], factors_f[0])
        + lifted(parts[0], factors_f[2])
        + lifted(parts[3], factors_f[1])
        + lifted(parts[1], factors_f[3])
    )
    normed_feature_adjoint = normed_feature_adjoint + adapter_scale * adjoint_contribution
    normed_feature_adjoint_direction = (
        normed_feature_adjoint_direction + adapter_scale * tangent_contribution
    )
    spread = (((0,), (1,)), ((), ()))
    gate_dir_rows = adjoints[2 * rank_size : 3 * rank_size]
    up_dir_rows = adjoints[3 * rank_size : 4 * rank_size]
    rank_row_values = adjoints[4 * rank_size : 5 * rank_size]
    gate_contribution = adapter_scale * lax.dot_general(
        normed_f, gate_dir_rows, spread, precision=lax.Precision.HIGHEST
    )
    up_contribution = adapter_scale * lax.dot_general(
        normed_f, up_dir_rows, spread, precision=lax.Precision.HIGHEST
    )
    down_contribution = adapter_scale * jnp.dot(
        rank_row_values, cotangent_float, precision=lax.Precision.HIGHEST
    )
    return (
        normed_feature_adjoint,
        normed_feature_adjoint_direction,
        gate_contribution,
        curvature_gate_output,
        up_contribution,
        curvature_up_output,
        curvature_down_input,
        down_contribution,
    )


def solution(mesh):
    in_specs = (
        P("col", "row"),
        P("row"),
        P("col", "row"),
        P("row", "col"),
        P("row", "col"),
        P("col", "row"),
        P("row", None),
        P(None, "col"),
        P("row", None),
        P(None, "col"),
        P("col", None),
        P(None, "row"),
        P("row", None),
        P(None, "col"),
        P("row", None),
        P(None, "col"),
        P("col", None),
        P(None, "row"),
    )
    out_specs = (
        P("col", "row"),
        P("col", "row"),
        P("row", None),
        P(None, "col"),
        P("row", None),
        P(None, "col"),
        P("col", None),
        P(None, "row"),
    )
    return jax.shard_map(
        on_device, mesh=mesh, in_specs=in_specs, out_specs=out_specs, check_vma=False
    )
```

profile of v0, /device:TPU:0, one launch (start us, length us, event | category | flops | bytes accessed | tf_op | source)
XLA Modules:
  0.0 468.7 jit_solution(18091516543193688266)
XLA Ops:
  8.3 11.4 %psum.28 = f32[32]{0:T(128)S(1)} all-reduce(f32[32]{0:T(128)S(1)} %fusion.49), channel_id=1, replica_groups=mesh['row'=4,'col'=8] {'row'}, use_global_device_ids=true, to_apply=%region_1.0 | all-reduce | flops 32 | bytes 256 | tf_op jit(solution)/shard_map/psum | solution.py:99
  22.2 21.0 %all-gather.3.cloned.1.call-done = bf16[256,2048]{1,0:T(8,128)(2,1)} async-done(((bf16[32,2048]{1,0:T(8,128)(2,1)}), bf16[256,2048]{1,0:T(8,128)(2,1)}) %all-gather.3.cloned.1.call-update) | async-done | bytes 1048592 | tf_op jit(solution)/shard_map/all_gather | solution.py:104
  43.2 11.5 %fusion.88 = f32[256,3584]{1,0:T(8,128)} fusion(bf16[256,2048]{1,0:T(8,128)(2,1)} %all-gather.3.cloned.1.call-done, bf16[2048,3584]{1,0:T(8,128)(2,1)} %param.21), kind=kOutput, calls=%fused_computation.126 | convolution fusion | flops 3758096384 | bytes 19398656 | tf_op jit(solution)/shard_map/dot_general | solution.py:12
  54.6 9.2 %fusion.89 = f32[256,3584]{1,0:T(8,128)} fusion(bf16[256,2048]{1,0:T(8,128)(2,1)S(1)} %copy-done.10, bf16[2048,3584]{1,0:T(8,128)(2,1)} %param.22), kind=kOutput, calls=%fused_computation.127 | convolution fusion | flops 3758096384 | bytes 19398656 | tf_op jit(solution)/shard_map/dot_general | solution.py:12
  63.8 2.8 all-gather.5.cloned.1.call-done
  66.6 11.4 %fusion.90 = f32[256,3584]{1,0:T(8,128)} fusion(bf16[256,2048]{1,0:T(8,128)(2,1)} %all-gather.5.cloned.1.call-done, bf16[3584,2048]{1,0:T(8,128)(2,1)} %param.23), kind=kOutput, calls=%fused_computation.128 | convolution fusion | flops 3758096384 | bytes 19398656 | tf_op jit(solution)/shard_map/dot_general | solution.py:16
  78.0 7.5 %pad_maximum_fusion = f32[256,10752]{1,0:T(8,128)} fusion(f32[256,3584]{1,0:T(8,128)} %fusion.90, f32[256,3584]{1,0:T(8,128)} %fusion.89, f32[256,3584]{1,0:T(8,128)S(1)} %copy-done.17), kind=kLoop, calls=%fused_computation | loop fusion | flops 5505024 | bytes 22020096 | tf_op jit(solution)/shard_map/concatenate | solution.py:123
  89.9 35.4 %all-reduce.7 = bf16[256,384]{0,1:T(8,128)(2,1)S(1)} all-reduce(f32[256,384]{0,1:T(8,128)S(1)} %pad_maximum_fusion.2), channel_id=1, replica_groups=mesh['row'=4,'col'=8] {'row'}, use_global_device_ids=true, to_apply=%region_3.0 | all-reduce | flops 98304 | bytes 589824 | tf_op jit(solution)/shard_map/psum | solution.py:121
  126.6 2.5 fusion.61
  129.1 2.5 fusion
  131.6 2.5 fusion.2
  134.1 178.0 %all-reduce.4.cloned.1.call-done = f32[256,10752]{1,0:T(8,128)} async-done(((f32[256,10752]{1,0:T(8,128)}), f32[256,10752]{1,0:T(8,128)}) %all-reduce.4.cloned.1.call-update) | async-done | bytes 11010064 | tf_op jit(solution)/shard_map/psum | solution.py:122
  312.1 4.5 fusion.3
  316.6 4.7 %fusion.5 = f32[256,3584]{1,0:T(8,128)} fusion(bf16[3584,64]{0,1:T(8,128)(2,1)S(1)} %copy-done.12, f32[256,10752]{1,0:T(8,128)} %all-reduce.4.cloned.1.call-done, bf16[256,384]{0,1:T(8,128)(2,1)S(1)} %all-reduce.7), kind=kOutput, calls=%fused_computation.12 | convolution fusion | flops 119275520 | bytes 7831552 | tf_op jit(solution)/shard_map/dot_general | solution.py:16
  321.3 4.7 %fusion.4 = f32[256,3584]{1,0:T(8,128)} fusion(bf16[64,3584]{1,0:T(8,128)(2,1)S(1)} %copy-done.9, f32[256,10752]{1,0:T(8,128)} %all-reduce.4.cloned.1.call-done, bf16[256,384]{0,1:T(8,128)(2,1)S(1)} %all-reduce.7), kind=kOutput, calls=%fused_computation.10 | convolution fusion | flops 119275520 | bytes 7831552 | tf_op jit(solution)/shard_map/dot_general | solution.py:12
  326.5 9.5 %add_convert_fusion = (bf16[256,3584]{1,0:T(8,128)(2,1)}, bf16[256,3584]{1,0:T(8,128)(2,1)S(1)}, bf16[256,3584]{1,0:T(8,128)(2,1)}, bf16[256,3584]{1,0:T(8,128)(...) fusion(f32[256,3584]{1,0:T(8,128)} %fusion.4, f32[256,3584]{1,0:T(8,128)S(1)} %copy-done.15, ...), kind=kOutput, calls=%fused_computation.31 | convolution fusion | flops 155975680 | bytes 33521664 | tf_op jit(solution)/shard_map/dot_general | solution.py:12
  337.9 8.6 %fusion.91 = f32[256,2048]{1,0:T(8,128)} fusion(bf16[256,3584]{1,0:T(8,128)(2,1)S(1)} %get-tuple-element.11, bf16[2048,3584]{1,0:T(8,128)(2,1)} %param.21), kind=kOutput, calls=%fused_computation.129 | convolution fusion | flops 3758096384 | bytes 18612224 | tf_op jit(solution)/shard_map/dot_general | solution.py:16
  347.2 8.7 %fusion.92 = f32[256,2048]{1,0:T(8,128)} fusion(bf16[256,3584]{1,0:T(8,128)(2,1)S(1)} %get-tuple-element.9, bf16[2048,3584]{1,0:T(8,128)(2,1)} %param.21), kind=kOutput, calls=%fused_computation.130 | convolution fusion | flops 3758096384 | bytes 18612224 | tf_op jit(solution)/shard_map/dot_general | solution.py:16
  355.9 2.2 fusion.94
  365.8 10.3 %fusion.19 = bf16[256,2048]{1,0:T(8,128)(2,1)S(1)} fusion(f32[256,2048]{1,0:T(8,128)} %fusion.91, bf16[256,3584]{1,0:T(8,128)(2,1)} %copy-done.1, bf16[2048,3584]{1,0:T(8,128)(2,1)} %param.22), kind=kOutput, calls=%fused_computation.39 | convolution fusion | flops 3759144960 | bytes 19660800 | tf_op jit(solution)/shard_map/dot_general | solution.py:16
  376.1 11.3 %fusion.20 = bf16[256,2048]{1,0:T(8,128)(2,1)} fusion(f32[256,2048]{1,0:T(8,128)} %fusion.92, bf16[256,3584]{1,0:T(8,128)(2,1)} %get-tuple-element.10, bf16[2048,3584]{1,0:T(8,128)(2,1)} %param.22), kind=kOutput, calls=%fused_computation.40 | convolution fusion | flops 3759144960 | bytes 19660800 | tf_op jit(solution)/shard_map/dot_general | solution.py:16
  387.4 2.8 pad_maximum_fusion.1
  397.4 20.9 %all-reduce.6.cloned.1.call-done = bf16[320,256]{1,0:T(8,128)(2,1)} async-done(((bf16[320,256]{1,0:T(8,128)(2,1)}), bf16[320,256]{1,0:T(8,128)(2,1)}) %all-reduce.6.cloned.1.call-update) | async-done | bytes 163856 | tf_op jit(solution)/shard_map/psum | solution.py:225
  426.8 31.5 %reduce-scatter.2.cloned.1.call-done = bf16[32,4096]{1,0:T(8,128)(2,1)} async-done(((bf16[256,4096]{1,0:T(8,128)(2,1)}), bf16[32,4096]{1,0:T(8,128)(2,1)}) %reduce-scatter.2.cloned.1.call-update) | async-done | bytes 262160 | tf_op jit(solution)/shard_map/reduce_scatter | solution.py:233
  (101 shorter events, 39.3 us)
Async XLA Ops:
  7.2 318.9 %copy-start = (bf16[64,3584]{1,0:T(8,128)(2,1)S(1)}, bf16[64,3584]{1,0:T(8,128)(2,1)}, u32[]{:S(2)}) copy-start(bf16[64,3584]{1,0:T(8,128)(2,1)} %param.33) | copy-start | bytes 1376260
  7.2 36.0 %all-gather.3.cloned.1.call-start = ((), (), s32[]{:S(2)}) async-start(), calls=%async_computation.1 | async-start | bytes 1179648 | tf_op jit(solution)/shard_map/all_gather | solution.py:104
  21.4 45.2 %all-gather.5.cloned.1.call-start = ((), (), s32[]{:S(2)}) async-start(), calls=%async_computation.2 | async-start | bytes 1179648 | tf_op jit(solution)/shard_map/all_gather | solution.py:105
  22.1 289.9 %all-reduce.4.cloned.1.call-start = ((), (), s32[]{:S(2)}) async-start(), calls=%async_computation.3 | async-start | bytes 22020096 | tf_op jit(solution)/shard_map/psum | solution.py:122
  43.2 11.5 %copy-start.10 = (bf16[256,2048]{1,0:T(8,128)(2,1)S(1)}, bf16[256,2048]{1,0:T(8,128)(2,1)}, u32[]{:S(2)}) copy-start(bf16[256,2048]{1,0:T(8,128)(2,1)} %all-gather.3.cloned.1.call-done) | copy-start | bytes 3145732
  66.6 11.4 %copy-start.17 = (f32[256,3584]{1,0:T(8,128)S(1)}, f32[256,3584]{1,0:T(8,128)}, u32[]{:S(2)}) copy-start(f32[256,3584]{1,0:T(8,128)} %fusion.88) | copy-start | bytes 11010052
  85.6 332.7 %all-reduce.6.cloned.1.call-start = ((), (), s32[]{:S(2)}) async-start(), calls=%async_computation.5 | async-start | bytes 327680 | tf_op jit(solution)/shard_map/psum | solution.py:225
  88.3 36.9 %copy-start.8 = (bf16[64,3584]{1,0:T(8,128)(2,1)S(1)}, bf16[64,3584]{1,0:T(8,128)(2,1)}, u32[]{:S(2)}) copy-start(bf16[64,3584]{1,0:T(8,128)(2,1)} %param.25) | copy-start | bytes 1376260
  89.8 36.1 %copy-start.12 = (bf16[3584,64]{0,1:T(8,128)(2,1)S(1)}, bf16[3584,64]{0,1:T(8,128)(2,1)}, u32[]{:S(2)}) copy-start(bf16[3584,64]{0,1:T(8,128)(2,1)} %param.28) | copy-start | bytes 1376260
  316.6 9.5 %copy-start.16 = (f32[256,3584]{1,0:T(8,128)S(1)}, f32[256,3584]{1,0:T(8,128)}, u32[]{:S(2)}) copy-start(f32[256,3584]{1,0:T(8,128)} %fusion.2) | copy-start | bytes 11010052
  321.3 4.7 %copy-start.14 = (f32[256,3584]{1,0:T(8,128)S(1)}, f32[256,3584]{1,0:T(8,128)}, u32[]{:S(2)}) copy-start(f32[256,3584]{1,0:T(8,128)} %fusion.61) | copy-start | bytes 11010052
  321.3 5.2 %copy-start.15 = (f32[256,3584]{1,0:T(8,128)S(1)}, f32[256,3584]{1,0:T(8,128)}, u32[]{:S(2)}) copy-start(f32[256,3584]{1,0:T(8,128)} %fusion) | copy-start | bytes 11010052
  336.1 11.2 %copy-start.3 = (bf16[256,3584]{1,0:T(8,128)(2,1)}, bf16[256,3584]{1,0:T(8,128)(2,1)S(1)}, u32[]{:S(2)}) copy-start(bf16[256,3584]{1,0:T(8,128)(2,1)S(1)} %get-tuple-element.9) | copy-start | bytes 5505028
  336.1 26.9 %copy-start.1 = (bf16[256,3584]{1,0:T(8,128)(2,1)}, bf16[256,3584]{1,0:T(8,128)(2,1)S(1)}, u32[]{:S(2)}) copy-start(bf16[256,3584]{1,0:T(8,128)(2,1)S(1)} %get-tuple-element.12) | copy-start | bytes 5505028
  347.2 10.9 %copy-start.13 = (bf16[3584,64]{0,1:T(8,128)(2,1)S(1)}, bf16[3584,64]{0,1:T(8,128)(2,1)}, u32[]{:S(2)}) copy-start(bf16[3584,64]{0,1:T(8,128)(2,1)} %param.28) | copy-start | bytes 1376260
  355.9 5.7 %copy-start.19 = (bf16[64,3584]{1,0:T(8,128)(2,1)S(1)}, bf16[64,3584]{1,0:T(8,128)(2,1)}, u32[]{:S(2)}) copy-start(bf16[64,3584]{1,0:T(8,128)(2,1)} %param.31) | copy-start | bytes 1376260
  360.3 3.9 copy-start.6
  360.3 3.9 copy-start.21
  365.5 92.7 %reduce-scatter.2.cloned.1.call-start = ((), (), s32[]{:S(2)}) async-start(), calls=%async_computation.4 | async-start | bytes 2359296 | tf_op jit(solution)/shard_map/reduce_scatter | solution.py:233
  394.6 23.7 %copy-start.25 = (bf16[2048,64]{0,1:T(8,128)(2,1)S(1)}, bf16[2048,64]{0,1:T(8,128)(2,1)}, u32[]{:S(2)}) copy-start(bf16[2048,64]{0,1:T(8,128)(2,1)} %param.24) | copy-start | bytes 786436
  396.0 25.6 %copy-start.23 = (bf16[2048,64]{0,1:T(8,128)(2,1)S(1)}, bf16[2048,64]{0,1:T(8,128)(2,1)}, u32[]{:S(2)}) copy-start(bf16[2048,64]{0,1:T(8,128)(2,1)} %param.26) | copy-start | bytes 786436
  396.0 26.7 %copy-start.11 = (bf16[256,2048]{1,0:T(8,128)(2,1)S(1)}, bf16[256,2048]{1,0:T(8,128)(2,1)}, u32[]{:S(2)}) copy-start(bf16[256,2048]{1,0:T(8,128)(2,1)} %all-gather.3.cloned.1.call-done) | copy-start | bytes 3145732
  397.4 28.2 %copy-start.27 = (bf16[256,2048]{1,0:T(8,128)(2,1)S(1)}, bf16[256,2048]{1,0:T(8,128)(2,1)}, u32[]{:S(2)}) copy-start(bf16[256,2048]{1,0:T(8,128)(2,1)} %all-gather.5.cloned.1.call-done) | copy-start | bytes 3145732
  418.3 6.2 %copy-start.29 = (bf16[320,256]{1,0:T(8,128)(2,1)S(1)}, bf16[320,256]{1,0:T(8,128)(2,1)}, u32[]{:S(2)}) copy-start(bf16[320,256]{1,0:T(8,128)(2,1)} %all-reduce.6.cloned.1.call-done) | copy-start | bytes 491524
  (11 other events, 26.3 us)
Sparse Core Ops, SparseCore 0:
  21.5 21.6 all-gather.2
  44.8 21.8 all-gather.4
  85.7 226.3 all-reduce.3
  365.7 52.6 all-reduce.5
  420.5 37.6 reduce-scatter.1
where the time goes:
time: 469 us
  waiting for transfers between devices  255 us (54%)
  matrix products  137 us (29%)
  blocking collectives  46.8 us (10%)
  other arithmetic  14.1 us (3%)
  between operations  14.1 us (3%)
    psum x1, waiting for transfers between devices, on_device(): lax.psum(jnp.concatenate([curvature_product(normed_tokens, gate_frozen_we...  178 us
    dot_general x15, matrix products, cross_shard_total(): lax.dot_general(left, right, (((1,), (1,)), ((), ())), preferred_element_...  68.3 us
    dot_general x9, matrix products, curvature_product(): return jnp.dot(left, right, preferred_element_type=jnp.float32)  46.5 us
    psum x1, blocking collectives, on_device(): ranks = lax.psum(projected, 'row').astype(jnp.bfloat16)  35.4 us
    reduce_scatter x1, waiting for transfers between devices, on_device(): lax.psum_scatter(jnp.concatenate([adjoint_contribution, tangent_contribut...  31.5 us
    all_gather x1, waiting for transfers between devices, on_device(): lax.all_gather(own_normed, 'col', axis=0, tiled=True)  21 us
    psum x1, waiting for transfers between devices, on_device(): lax.psum(rank_adjoints.astype(jnp.bfloat16), 'col').astype(jnp.float32)  20.9 us
    psum x1, blocking collectives, on_device(): squares = lax.psum(jnp.sum(tokens_f * tokens_f, axis=1), 'row')  11.4 us
  transfers between devices with their start and end apart: 5, of which 5 were waited for; matrix products, arithmetic and copies ran while one was open for 15% of the time, Pallas kernels for 0%

commit v1 on v0

--- a/solution.py
+++ b/solution.py
@@ -119,16 +119,19 @@
         axis=1,
     )
     ranks = lax.psum(projected, "row").astype(jnp.bfloat16)
-    swiglu_block = lax.psum(
-        jnp.concatenate(
-            [
-                curvature_product(normed_tokens, gate_frozen_weight),
-                curvature_product(normed_tokens, up_frozen_weight),
-                cross_shard_total(cot_panel, down_frozen_weight),
-            ],
-            axis=1,
+    swiglu_block = jnp.sum(
+        lax.all_gather(
+            jnp.concatenate(
+                [
+                    curvature_product(normed_tokens, gate_frozen_weight),
+                    curvature_product(normed_tokens, up_frozen_weight),
+                    cross_shard_total(cot_panel, down_frozen_weight),
+                ],
+                axis=1,
+            ),
+            "row",
         ),
-        "row",
+        axis=0,
     )
 
     def column(array, index):

time: 469 us -> 652 us (1.39)
  waiting for transfers between devices: 255 us -> 417 us
  other arithmetic: 14.1 us -> 34.4 us
    all_gather x0 -> x1, waiting for transfers between devices: none -> 344 us  [on_device(): lax.all_gather(jnp.concatenate([curvature_product(normed_tokens, gate_fro...]
    psum x1 -> x0, waiting for transfers between devices: 178 us -> none  [on_device(): lax.psum(jnp.concatenate([curvature_product(normed_tokens, gate_frozen_we...]
    reduce_sum x0 -> x1, other arithmetic: none -> 20.3 us  [on_device(): jnp.sum(lax.all_gather(jnp.concatenate([curvature_product(normed_tokens,...]
  transfers between devices with their start and end apart: 5 -> 5, of which waited for: 5 -> 5; matrix products, arithmetic and copies ran while one was open for 15% -> 12% of each run, Pallas kernels for 0% -> 0%
where the time goes in v1:
time: 652 us; the launch traced here: 651 us
  waiting for transfers between devices  417 us (64%)
  matrix products  143 us (22%)
  blocking collectives  40.3 us (6%)
  other arithmetic  34.4 us (5%)
  between operations  14.1 us (2%)
    all_gather x1, waiting for transfers between devices, on_device(): lax.all_gather(jnp.concatenate([curvature_product(normed_tokens, gate_fro...  344 us
    dot_general x15, matrix products, cross_shard_total(): lax.dot_general(left, right, (((1,), (1,)), ((), ())), preferred_element_...  74.8 us
    dot_general x9, matrix products, curvature_product(): return jnp.dot(left, right, preferred_element_type=jnp.float32)  46.4 us
    reduce_scatter x1, waiting for transfers between devices, on_device(): lax.psum_scatter(jnp.concatenate([adjoint_contribution, tangent_contribut...  31.4 us
    psum x1, blocking collectives, on_device(): ranks = lax.psum(projected, 'row').astype(jnp.bfloat16)  28.9 us
    all_gather x1, waiting for transfers between devices, on_device(): lax.all_gather(own_normed, 'col', axis=0, tiled=True)  21 us
    reduce_sum x1, other arithmetic, on_device(): jnp.sum(lax.all_gather(jnp.concatenate([curvature_product(normed_tokens,...  20.3 us
    psum x1, waiting for transfers between devices, on_device(): lax.psum(rank_adjoints.astype(jnp.bfloat16), 'col').astype(jnp.float32)  16.6 us
  transfers between devices with their start and end apart: 5, of which 5 were waited for; matrix products, arithmetic and copies ran while one was open for 12% of the time, Pallas kernels for 0%

profile of v1, /device:TPU:0, one launch (start us, length us, event | category | flops | bytes accessed | tf_op | source)
XLA Modules:
  0.0 651.4 jit_solution(5762324495696623502)
XLA Ops:
  8.3 11.4 %psum.21 = f32[32]{0:T(128)S(1)} all-reduce(f32[32]{0:T(128)S(1)} %fusion.49), channel_id=1, replica_groups=mesh['row'=4,'col'=8] {'row'}, use_global_device_ids=true, to_apply=%region_1.0 | all-reduce | flops 32 | bytes 256 | tf_op jit(solution)/shard_map/psum | solution.py:99
  22.2 21.0 %all-gather.5.cloned.1.call-done = bf16[256,2048]{1,0:T(8,128)(2,1)} async-done(((bf16[32,2048]{1,0:T(8,128)(2,1)}), bf16[256,2048]{1,0:T(8,128)(2,1)}) %all-gather.5.cloned.1.call-update) | async-done | bytes 1048592 | tf_op jit(solution)/shard_map/all_gather | solution.py:104
  43.2 11.5 %fusion.89 = f32[256,3584]{1,0:T(8,128)} fusion(bf16[256,2048]{1,0:T(8,128)(2,1)} %all-gather.5.cloned.1.call-done, bf16[2048,3584]{1,0:T(8,128)(2,1)} %param.22), kind=kOutput, calls=%fused_computation.127 | convolution fusion | flops 3758096384 | bytes 19398656 | tf_op jit(solution)/shard_map/dot_general | solution.py:12
  54.6 9.1 %fusion.88 = f32[256,3584]{1,0:T(8,128)} fusion(bf16[256,2048]{1,0:T(8,128)(2,1)S(1)} %copy-done.10, bf16[2048,3584]{1,0:T(8,128)(2,1)} %param.21), kind=kOutput, calls=%fused_computation.126 | convolution fusion | flops 3758096384 | bytes 19398656 | tf_op jit(solution)/shard_map/dot_general | solution.py:12
  63.8 2.8 all-gather.7.cloned.1.call-done
  66.6 11.4 %fusion.90 = f32[256,3584]{1,0:T(8,128)} fusion(bf16[256,2048]{1,0:T(8,128)(2,1)} %all-gather.7.cloned.1.call-done, bf16[3584,2048]{1,0:T(8,128)(2,1)} %param.23), kind=kOutput, calls=%fused_computation.128 | convolution fusion | flops 3758096384 | bytes 19398656 | tf_op jit(solution)/shard_map/dot_general | solution.py:16
  78.0 7.5 %pad_maximum_fusion = f32[256,10752]{1,0:T(8,128)} fusion(f32[256,3584]{1,0:T(8,128)} %fusion.90, f32[256,3584]{1,0:T(8,128)S(1)} %copy-done.16, f32[256,3584]{1,0:T(8,128)} %fusion.88), kind=kLoop, calls=%fused_computation | loop fusion | flops 5505024 | bytes 22020096 | tf_op jit(solution)/shard_map/concatenate | solution.py:124
  89.9 28.9 %all-reduce.4 = bf16[256,384]{0,1:T(8,128)(2,1)S(1)} all-reduce(f32[256,384]{0,1:T(8,128)S(1)} %pad_maximum_fusion.2), channel_id=1, replica_groups=mesh['row'=4,'col'=8] {'row'}, use_global_device_ids=true, to_apply=%region_3.0 | all-reduce | flops 98304 | bytes 589824 | tf_op jit(solution)/shard_map/psum | solution.py:121
  120.2 2.4 fusion.61
  122.6 2.4 fusion
  125.1 2.5 fusion.2
  127.6 343.9 %all-gather.9.cloned.1.call-done = f32[1024,10752]{1,0:T(8,128)} async-done(((f32[256,10752]{1,0:T(8,128)}), f32[1024,10752]{1,0:T(8,128)}) %all-gather.9.cloned.1.call-update) | async-done | bytes 44040208 | tf_op jit(solution)/shard_map/all_gather | solution.py:123
  471.4 20.3 %reduce_sum.19 = f32[256,10752]{1,0:T(8,128)} reduce(f32[4,256,10752]{2,1,0:T(8,128)} %bitcast.79, f32[]{:T(128)} %constant.10.clone.1), dimensions={0}, to_apply=%region_2.0 | reduce | flops 8257536 | bytes 55050244 | tf_op jit(solution)/shard_map/reduce_sum | solution.py:122
  491.8 4.5 fusion.4
  496.3 4.5 fusion.3
  500.8 4.8 fusion.5
  506.0 9.7 %add_convert_fusion = (bf16[256,3584]{1,0:T(8,128)(2,1)}, bf16[256,3584]{1,0:T(8,128)(2,1)S(1)}, bf16[256,3584]{1,0:T(8,128)(2,1)}, bf16[256,3584]{1,0:T(8,128)(...) fusion(f32[256,3584]{1,0:T(8,128)} %fusion.4, f32[256,3584]{1,0:T(8,128)S(1)} %copy-done.15, ...), kind=kOutput, calls=%fused_computation.31 | convolution fusion | flops 155975680 | bytes 33521664 | tf_op jit(solution)/shard_map/dot_general | solution.py:12
  517.7 11.0 %fusion.92 = f32[256,2048]{1,0:T(8,128)} fusion(bf16[256,3584]{1,0:T(8,128)(2,1)} %copy-done.5, bf16[2048,3584]{1,0:T(8,128)(2,1)} %param.21), kind=kOutput, calls=%fused_computation.130 | convolution fusion | flops 3758096384 | bytes 18612224 | tf_op jit(solution)/shard_map/dot_general | solution.py:16
  530.0 8.7 %fusion.91 = f32[256,2048]{1,0:T(8,128)} fusion(bf16[256,3584]{1,0:T(8,128)(2,1)S(1)} %get-tuple-element.11, bf16[2048,3584]{1,0:T(8,128)(2,1)} %param.21), kind=kOutput, calls=%fused_computation.129 | convolution fusion | flops 3758096384 | bytes 18612224 | tf_op jit(solution)/shard_map/dot_general | solution.py:16
  548.3 10.3 %fusion.20 = bf16[256,2048]{1,0:T(8,128)(2,1)S(1)} fusion(f32[256,2048]{1,0:T(8,128)} %fusion.92, bf16[256,3584]{1,0:T(8,128)(2,1)} %get-tuple-element.10, bf16[2048,3584]{1,0:T(8,128)(2,1)} %param.22), kind=kOutput, calls=%fused_computation.40 | convolution fusion | flops 3759144960 | bytes 19660800 | tf_op jit(solution)/shard_map/dot_general | solution.py:16
  558.6 15.9 %fusion.19 = bf16[256,2048]{1,0:T(8,128)(2,1)} fusion(f32[256,2048]{1,0:T(8,128)} %fusion.91, bf16[256,3584]{1,0:T(8,128)(2,1)S(1)} %get-tuple-element.12, bf16[2048,3584]{1,0:T(8,128)(2,1)} %param.22), kind=kOutput, calls=%fused_computation.39 | convolution fusion | flops 3759144960 | bytes 19660800 | tf_op jit(solution)/shard_map/dot_general | solution.py:16
  574.5 2.8 pad_maximum_fusion.1
  584.5 16.6 %all-reduce.3.cloned.1.call-done = bf16[320,256]{1,0:T(8,128)(2,1)} async-done(((bf16[320,256]{1,0:T(8,128)(2,1)}), bf16[320,256]{1,0:T(8,128)(2,1)}) %all-reduce.3.cloned.1.call-update) | async-done | bytes 163856 | tf_op jit(solution)/shard_map/psum | solution.py:228
  609.5 31.4 %reduce-scatter.2.cloned.1.call-done = bf16[32,4096]{1,0:T(8,128)(2,1)} async-done(((bf16[256,4096]{1,0:T(8,128)(2,1)}), bf16[32,4096]{1,0:T(8,128)(2,1)}) %reduce-scatter.2.cloned.1.call-update) | async-done | bytes 262160 | tf_op jit(solution)/shard_map/reduce_scatter | solution.py:236
  (100 shorter events, 41.9 us)
Async XLA Ops:
  7.2 498.4 %copy-start = (bf16[64,3584]{1,0:T(8,128)(2,1)S(1)}, bf16[64,3584]{1,0:T(8,128)(2,1)}, u32[]{:S(2)}) copy-start(bf16[64,3584]{1,0:T(8,128)(2,1)} %param.33) | copy-start | bytes 1376260
  7.2 36.0 %all-gather.5.cloned.1.call-start = ((), (), s32[]{:S(2)}) async-start(), calls=%async_computation.1 | async-start | bytes 1179648 | tf_op jit(solution)/shard_map/all_gather | solution.py:104
  21.4 45.2 %all-gather.7.cloned.1.call-start = ((), (), s32[]{:S(2)}) async-start(), calls=%async_computation.2 | async-start | bytes 1179648 | tf_op jit(solution)/shard_map/all_gather | solution.py:105
  22.1 449.3 %all-gather.9.cloned.1.call-start = ((), (), s32[]{:S(2)}) async-start(), calls=%async_computation.5 | async-start | bytes 55050240 | tf_op jit(solution)/shard_map/all_gather | solution.py:123
  43.2 11.5 %copy-start.10 = (bf16[256,2048]{1,0:T(8,128)(2,1)S(1)}, bf16[256,2048]{1,0:T(8,128)(2,1)}, u32[]{:S(2)}) copy-start(bf16[256,2048]{1,0:T(8,128)(2,1)} %all-gather.5.cloned.1.call-done) | copy-start | bytes 3145732
  66.6 11.4 %copy-start.16 = (f32[256,3584]{1,0:T(8,128)S(1)}, f32[256,3584]{1,0:T(8,128)}, u32[]{:S(2)}) copy-start(f32[256,3584]{1,0:T(8,128)} %fusion.89) | copy-start | bytes 11010052
  85.6 515.5 %all-reduce.3.cloned.1.call-start = ((), (), s32[]{:S(2)}) async-start(), calls=%async_computation.4 | async-start | bytes 327680 | tf_op jit(solution)/shard_map/psum | solution.py:228
  88.3 30.5 %copy-start.8 = (bf16[64,3584]{1,0:T(8,128)(2,1)S(1)}, bf16[64,3584]{1,0:T(8,128)(2,1)}, u32[]{:S(2)}) copy-start(bf16[64,3584]{1,0:T(8,128)(2,1)} %param.25) | copy-start | bytes 1376260
  89.8 29.7 %copy-start.12 = (bf16[3584,64]{0,1:T(8,128)(2,1)S(1)}, bf16[3584,64]{0,1:T(8,128)(2,1)}, u32[]{:S(2)}) copy-start(bf16[3584,64]{0,1:T(8,128)(2,1)} %param.28) | copy-start | bytes 1376260
  119.5 3.1 copy-start.17
  500.8 4.8 copy-start.14
  500.8 5.2 copy-start.15
  515.8 28.6 %copy-start.1 = (bf16[256,3584]{1,0:T(8,128)(2,1)}, bf16[256,3584]{1,0:T(8,128)(2,1)S(1)}, u32[]{:S(2)}) copy-start(bf16[256,3584]{1,0:T(8,128)(2,1)S(1)} %get-tuple-element.11) | copy-start | bytes 5505028
  515.8 31.2 %copy-start.2 = (bf16[256,3584]{1,0:T(8,128)(2,1)}, bf16[256,3584]{1,0:T(8,128)(2,1)S(1)}, u32[]{:S(2)}) copy-start(bf16[256,3584]{1,0:T(8,128)(2,1)S(1)} %get-tuple-element.13) | copy-start | bytes 5505028
  530.0 10.9 %copy-start.13 = (bf16[3584,64]{0,1:T(8,128)(2,1)S(1)}, bf16[3584,64]{0,1:T(8,128)(2,1)}, u32[]{:S(2)}) copy-start(bf16[3584,64]{0,1:T(8,128)(2,1)} %param.28) | copy-start | bytes 1376260
  538.6 5.7 copy-start.18
  543.0 3.9 copy-start.20
  548.2 92.7 %reduce-scatter.2.cloned.1.call-start = ((), (), s32[]{:S(2)}) async-start(), calls=%async_computation.3 | async-start | bytes 2359296 | tf_op jit(solution)/shard_map/reduce_scatter | solution.py:236
  577.3 3.0 copy-start.6
  581.7 19.4 %copy-start.24 = (bf16[2048,64]{0,1:T(8,128)(2,1)S(1)}, bf16[2048,64]{0,1:T(8,128)(2,1)}, u32[]{:S(2)}) copy-start(bf16[2048,64]{0,1:T(8,128)(2,1)} %param.24) | copy-start | bytes 786436
  583.1 21.3 %copy-start.22 = (bf16[2048,64]{0,1:T(8,128)(2,1)S(1)}, bf16[2048,64]{0,1:T(8,128)(2,1)}, u32[]{:S(2)}) copy-start(bf16[2048,64]{0,1:T(8,128)(2,1)} %param.26) | copy-start | bytes 786436
  583.1 22.4 %copy-start.11 = (bf16[256,2048]{1,0:T(8,128)(2,1)S(1)}, bf16[256,2048]{1,0:T(8,128)(2,1)}, u32[]{:S(2)}) copy-start(bf16[256,2048]{1,0:T(8,128)(2,1)} %all-gather.5.cloned.1.call-done) | copy-start | bytes 3145732
  584.5 24.0 %copy-start.26 = (bf16[256,2048]{1,0:T(8,128)(2,1)S(1)}, bf16[256,2048]{1,0:T(8,128)(2,1)}, u32[]{:S(2)}) copy-start(bf16[256,2048]{1,0:T(8,128)(2,1)} %all-gather.7.cloned.1.call-done) | copy-start | bytes 3145732
  601.1 6.2 copy-start.28
  (10 other events, 21.7 us)
Sparse Core Ops, SparseCore 0:
  21.5 21.6 all-gather.4
  44.8 21.8 all-gather.6
  85.7 385.6 all-gather.8
  548.4 52.6 all-reduce.2
  603.2 37.6 reduce-scatter.1
